TPU v7x, 128 devices: a whole 4x4x4 slice. The times are simulated.
128 devices in a mesh: ang: 8 (over x, core), det: 16 (over z, y).
Axes of the slice: x: 4, y: 4, z: 4, core: 2. Of those that a mesh axis runs over, the one named last changes fastest.
Arguments:
- raw_counts: float32 [256, 128, 4096], P('ang', None, 'det'), may hold values from 0.15 to 0.9
- dark_field: float32 [128, 4096], P(None, 'det'), may hold values from 0 to 0.1
- flat_field: float32 [128, 4096], P(None, 'det'), may hold values from 0.8 to 1.2
- destinations: int32 [32, 1], replicated, may hold values from 0 to 15; in each aligned block of 32 rows (0 to 31, 32 to 63, ...) at most 4 rows name the same one
- band_offsets: int32 [4096], replicated, may hold values from 0 to 4092, as said below
- band_weights: float32 [4, 4096], replicated, may hold values from 0.05 to 0.5
Outputs:
- parallel_slabs: float32 [256, 64, 4, 4096], P('ang', 'det')
Inputs may be any that keep to these rules, and one draw needn't show every extreme that they name: `destinations`: no z-slab owner receives more than 4 row blocks, and some owner receives exactly 4. band_offsets[t] lies between t - 8 and t + 5.
All inputs are finite; a program needn't handle non-finite values.
Results may differ from a plain program's by a relative error of at most 0.0001.
Values sent between devices are 32-bit elements; how exact they have to be, the bound alone decides.
A program may use at most 64 MiB of HBM per device.

v0:
```python
import jax
import jax.numpy as jnp
from jax import lax
from jax.sharding import PartitionSpec as P

RB = 4
SMW = 4
ITERS = 3
HB = 8
BW = 4
MOST = 4
cauchy_scale = 0.2


def with_halo(x, sides, width):
    for axis, dim in sides:
        count, length = (lax.axis_size(axis), x.shape[dim])
        up = [(i, (i + 1) % count) for i in range(count - 1)]
        down = [(j, i) for i, j in up]
        last = lax.slice_in_dim(x, length - width, length, axis=dim)
        leading = lax.slice_in_dim(x, 0, width, axis=dim)
        before = lax.ppermute(last, axis, up)
        after = lax.ppermute(leading, axis, down)
        x = jnp.concatenate([before, x, after], axis=dim)
    return x


def smooth_local(values, first_col, total_cols):
    col_width = values.shape[2]
    padded = with_halo(values, (("det", 2),), SMW)
    summed = padded[:, :, 0:col_width]
    for position in range(1, 2 * SMW + 1):
        summed = summed + padded[:, :, position : position + col_width]
    columns = first_col + jnp.arange(col_width, dtype=jnp.int32)
    counts = jnp.minimum(columns + SMW, total_cols - 1) - jnp.maximum(columns - SMW, 0) + 1
    return summed / counts.astype(jnp.float32)


def band_sum(widened, relative, weights, col_width):
    summed = None
    for shift in range(-HB, HB + 1):
        coeff = jnp.zeros((col_width,), jnp.float32)
        for position in range(BW):
            coeff = coeff + jnp.where(relative == shift - position, weights[position], 0.0)
        term = coeff * widened[..., HB + shift : HB + shift + col_width]
        summed = term if summed is None else summed + term
    return summed


def slot_tables(destinations, owners, most):
    targets = destinations[:, 0]
    block_ids = jnp.arange(targets.shape[0], dtype=jnp.int32)
    same_earlier = (targets[:, None] == targets[None, :]) & (
        block_ids[None, :] < block_ids[:, None]
    )
    slot_rank = jnp.sum(same_earlier.astype(jnp.int32), axis=1)
    owner_ids = jnp.arange(owners, dtype=jnp.int32)
    rank_ids = jnp.arange(most, dtype=jnp.int32)
    matching = (
        (targets[None, None, :] == owner_ids[:, None, None])
        & (slot_rank[None, None, :] == rank_ids[None, :, None])
    ).astype(jnp.int32)
    chosen = jnp.sum(matching * block_ids[None, None, :], axis=2)
    filled = jnp.sum(matching, axis=2)
    return (chosen, filled)


def slot_blocks(values, destinations, owners):
    ang_dev, row_count, col_width = values.shape
    blocks = values.reshape(ang_dev, row_count // RB, RB, col_width)
    chosen, filled = slot_tables(destinations, owners, MOST)
    picked = jnp.take(blocks, chosen.reshape(-1), axis=1).reshape(
        ang_dev, owners, MOST, RB, col_width
    )
    return picked * filled[None, :, :, None, None].astype(jnp.float32)


def body(raw_counts, dark_field, flat_field, destinations, band_offsets, band_weights):
    ang_dev, row_count, col_width = raw_counts.shape
    owners = lax.axis_size("det")
    first_col = lax.axis_index("det") * col_width
    total_cols = col_width * owners
    angles = ang_dev * lax.axis_size("ang")
    projected = -jnp.log((raw_counts - dark_field) / (flat_field - dark_field))
    detail = projected - smooth_local(projected, first_col, total_cols)
    gain_map = lax.psum(jnp.sum(detail, axis=0), "ang") / angles
    for reweight_pass in range(ITERS):
        scaled = (detail - gain_map) / cauchy_scale
        weights = 1.0 / (1.0 + scaled * scaled)
        weighted = jnp.sum(weights * detail, axis=0)
        weight_total = jnp.sum(weights, axis=0)
        total_all, weighted_all = lax.psum((weight_total, weighted), "ang")
        gain_map = weighted_all / total_all
    corrected = projected - gain_map
    picked = slot_blocks(corrected, destinations, owners)
    relative_all = band_offsets - jnp.arange(total_cols, dtype=jnp.int32)
    arrived = lax.all_to_all(picked, "det", split_axis=1, concat_axis=4, tiled=True)
    pad_widths = [(0, 0)] * (arrived.ndim - 1) + [(HB, HB)]
    widened_all = jnp.pad(arrived, pad_widths)
    moved = band_sum(widened_all, relative_all, band_weights, arrived.shape[-1])
    return moved.reshape(ang_dev, MOST, RB, total_cols)


def solution(mesh):
    placed = (P("ang", None, "det"), P(None, "det"), P(None, "det"), P(), P(), P())
    return jax.shard_map(
        body, mesh=mesh, in_specs=placed, out_specs=P("ang", "det", None, None), check_vma=False
    )
```

profile of v0, /device:TPU:6, one launch (start us, length us, event | category | flops | bytes accessed | tf_op | source)
XLA Modules:
  0.0 526.5 jit_solution(13446992526522736455)
XLA Ops:
  6.5 5.5 %copy.19 = f32[32,128,256]{1,0,2:T(8,128)} copy(f32[32,128,256]{2,1,0:T(8,128)} %param.6) | data formatting | bytes 8388608 | tf_op args[0]
  12.3 3.0 log_negate_fusion
  15.3 2.0 copy-done
  17.3 3.5 collective-permute-start
  20.8 1.3 collective-permute-start.1
  22.1 0.5 collective-permute-done
  22.6 4.3 collective-permute-done.1
  26.9 19.3 %fusion.36 = (f32[128,256]{0,1:T(8,128)}, f32[32,128,256]{1,0,2:T(8,128)}) fusion(f32[32,128,256]{1,0,2:T(8,128)} %copy-done, f32[256]{0:T(256)S(1)} %add_convert_fusion, f32[32,128,4]{1,0,2:T(8,128)S(1)} %collective-permute-done.1, f32[32,128,4]{1,0,2:T(8,128)S(1)} %collective-permute-done), kind=kLoop, calls=%fused_computation.112 | loop fusion | flops 19890176 | bytes 8651776 | tf_op jit(solution)/shard_map/reduce_sum | solution.py:86
  46.3 0.2 convert_reduce_fusion
  46.5 61.3 %all-reduce.9.cloned.1.call-done = f32[128,256]{0,1:T(8,128)} async-done(((f32[128,256]{0,1:T(8,128)}), f32[128,256]{0,1:T(8,128)}) %all-reduce.9.cloned.1.call-update) | async-done | bytes 131088 | tf_op jit(solution)/shard_map/psum | solution.py:86
  107.8 0.9 broadcast_multiply_fusion
  108.7 4.8 fusion.29
  113.6 0.2 fusion.33
  114.0 59.1 %all-reduce.15.cloned.1.call-done = (f32[128,256]{0,1:T(8,128)}, f32[128,256]{0,1:T(8,128)}) async-done(((f32[128,256]{0,1:T(8,128)}, f32[128,256]{0,1:T(8,128)}), (f32[128,256]{0,1:T(8,128)}, f32[128,256]{0,1:T(8,128)})) %all-reduce.15.cloned.1.call-update) | async-done | bytes 262160 | tf_op jit(solution)/shard_map/psum | solution.py:92
  173.1 1.0 div.57
  174.1 4.8 fusion.30
  179.0 0.2 all-reduce.11.cloned.1.call-start
  179.2 59.4 %all-reduce.13.cloned.1.call-done = (f32[128,256]{0,1:T(8,128)}, f32[128,256]{0,1:T(8,128)}) async-done(((f32[128,256]{0,1:T(8,128)}, f32[128,256]{0,1:T(8,128)}), (f32[128,256]{0,1:T(8,128)}, f32[128,256]{0,1:T(8,128)})) %all-reduce.13.cloned.1.call-update) | async-done | bytes 262160 | tf_op jit(solution)/shard_map/psum | solution.py:92
  238.6 1.0 div.60
  239.6 4.8 fusion.31
  244.4 0.1 copy.17
  244.6 59.5 %all-reduce.11.cloned.1.call-done = (f32[128,256]{0,1:T(8,128)}, f32[128,256]{0,1:T(8,128)}) async-done(((f32[128,256]{0,1:T(8,128)}, f32[128,256]{0,1:T(8,128)}), (f32[128,256]{0,1:T(8,128)}, f32[128,256]{0,1:T(8,128)})) %all-reduce.11.cloned.1.call-update) | async-done | bytes 262160 | tf_op jit(solution)/shard_map/psum | solution.py:92
  304.1 1.0 div.63
  305.1 5.4 %broadcast_subtract_fusion = f32[32,128,256]{1,0,2:T(8,128)} fusion(f32[128,256]{0,1:T(8,128)S(1)} %div.63, f32[128,256]{0,1:T(8,128)S(1)} %copy.20, f32[32,128,256]{1,0,2:T(8,128)} %copy.19, f32[128,256]{0,1:T(8,128)S(1)} %copy.18), kind=kLoop, calls=%fused_computation.59 | loop fusion | flops 4194304 | bytes 8781824 | tf_op jit(solution)/shard_map/sub | solution.py:94
  310.5 5.6 %copy.21 = f32[32,128,256]{2,0,1:T(8,128)} copy(f32[32,128,256]{1,0,2:T(8,128)} %broadcast_subtract_fusion) | data formatting | bytes 8388608 | tf_op jit(solution)/shard_map/sub | solution.py:94
  316.1 6.7 %gather_fusion = f32[64,32,4,256]{3,1,2,0:T(8,128)} fusion(f32[32,32,4,256]{3,0,2,1:T(8,128)} %bitcast.18, s32[1024]{0:T(1024)S(1)} %pad_clamp_fusion), kind=kCustom, calls=%fused_computation | custom fusion | bytes 16777472 | tf_op jit(solution)/shard_map/jit(_take)/gather | solution.py:72
  322.8 8.9 %select_multiply_fusion = f32[32,16,4,4,256]{4,0,3,2,1:T(8,128)} fusion(f32[32,16,4,4,256]{4,0,3,2,1:T(8,128)} %bitcast.20, f32[16,4]{1,0:T(8,128)S(1)} %copy.23, pred[16,4]{1,0:T(8,128)(4,1)S(1)} %copy.17), kind=kLoop, calls=%fused_computation.22 | loop fusion | flops 4194304 | bytes 16777536 | tf_op jit(solution)/shard_map/mul | solution.py:75
  331.6 7.2 %all-to-all-start = ((f32[32,16,4,4,256]{4,0,3,2,1:T(8,128)}), f32[32,16,4,4,256]{4,0,3,2,1:T(8,128)}, u32[]{:S(2)}, u32[]{:S(2)}) async-start(f32[32,16,4,4,256]{4,0,3,2,1:T(8,128)} %select_multiply_fusion), calls=%async_computation | async-start | bytes 16777216 | tf_op jit(solution)/shard_map/all_to_all | solution.py:97
  339.0 127.9 %all-to-all-done = f32[32,16,4,4,256]{4,0,3,2,1:T(8,128)} async-done(((f32[32,16,4,4,256]{4,0,3,2,1:T(8,128)}), f32[32,16,4,4,256]{4,0,3,2,1:T(8,128)}, u32[]{:S(2)}, u32[]{:S(2)}) %all-to-all-start) | async-done | bytes 8388640 | tf_op jit(solution)/shard_map/all_to_all | solution.py:97
  466.8 4.6 copy.26
  471.5 36.4 %add_bitcast_fusion = f32[32,4,4,4096]{3,0,2,1:T(8,128)} fusion(f32[32,1,4,4,4096]{4,0,3,2,1:T(8,128)S(1)} %bitcast.19, f32[4096]{0:T(1024)S(1)} %get-tuple-element.24, f32[4096]{0:T(1024)S(1)} %get-tuple-element.25, f32[4096]{0:T(1024)S(1)} %get-tuple-element.26, f32[4096]{0:T(1024)S(1)} %get-tuple-element.27, f32[4096]{0:T(1024)S(1)} %get-tuple-element.28, ...), kind=kLoop, calls=%fused_computation.1 | loop fusion | flops 69206016 | bytes 17055744 | tf_op jit(solution)/shard_map/reshape | solution.py:101
  507.8 12.2 %copy.25 = f32[32,4,4,4096]{3,2,1,0:T(4,128)} copy(f32[32,4,4,4096]{3,0,2,1:T(8,128)} %add_bitcast_fusion) | data formatting | bytes 16777216 | tf_op jit(solution)/shard_map/reshape | solution.py:101
  (34 shorter events, 0.8 us)
Async XLA Ops:
  6.5 5.5 %copy-start.1 = (f32[128,256]{1,0:T(8,128)S(1)}, f32[128,256]{1,0:T(8,128)}, u32[]{:S(2)}) copy-start(f32[128,256]{1,0:T(8,128)} %param.7) | copy-start | bytes 393220
  6.5 5.6 %copy-start.2 = (f32[128,256]{1,0:T(8,128)S(1)}, f32[128,256]{1,0:T(8,128)}, u32[]{:S(2)}) copy-start(f32[128,256]{1,0:T(8,128)} %param.8) | copy-start | bytes 393220
  6.5 101.3 %all-reduce.9.cloned.1.call-start = ((), (), s32[]{:S(2)}) async-start(), calls=%async_computation.1 | async-start | bytes 262144 | tf_op jit(solution)/shard_map/psum | solution.py:86
  12.2 9.8 %copy-start.5 = (s32[32,1]{0,1:T(1,128)S(1)}, s32[32,1]{0,1:T(1,128)}, u32[]{:S(2)}) copy-start(s32[32,1]{0,1:T(1,128)} %param.9) | copy-start | bytes 388
  15.3 2.0 copy-start
  17.3 5.4 %collective-permute-start = (f32[32,128,4]{1,0,2:T(8,128)S(1)}, f32[32,128,4]{1,0,2:T(8,128)S(1)}, u32[]{:S(2)}, u32[]{:S(2)}) collective-permute-start(f32[32,128,4]{1,0,2:T(8,128)S(1)} %get-tuple-element.21), channel_id=1, source_target_pairs={{0,1},{1,2},{2,3},{3,4},{4,5},{5,6},{6,7},{7,8},{8,9},{9,10},{10,1... | collective-permute-start | bytes 196616 | tf_op jit(solution)/shard_map/ppermute | solution.py:22
  20.8 6.2 %collective-permute-start.1 = (f32[32,128,4]{1,0,2:T(8,128)S(1)}, f32[32,128,4]{1,0,2:T(8,128)S(1)}, u32[]{:S(2)}, u32[]{:S(2)}) collective-permute-start(f32[32,128,4]{1,0,2:T(8,128)S(1)} %get-tuple-element.22), channel_id=1, source_target_pairs={{1,0},{2,1},{3,2},{4,3},{5,4},{6,5},{7,6},{8,7},{9,8},{10,9},{11,1... | collective-permute-start | bytes 196616 | tf_op jit(solution)/shard_map/ppermute | solution.py:23
  46.2 126.9 %all-reduce.15.cloned.1.call-start = ((), (), s32[]{:S(2)}) async-start(), calls=%async_computation.4 | async-start | bytes 524288 | tf_op jit(solution)/shard_map/psum | solution.py:92
  113.5 125.0 %all-reduce.13.cloned.1.call-start = ((), (), s32[]{:S(2)}) async-start(), calls=%async_computation.3 | async-start | bytes 524288 | tf_op jit(solution)/shard_map/psum | solution.py:92
  179.0 125.1 %all-reduce.11.cloned.1.call-start = ((), (), s32[]{:S(2)}) async-start(), calls=%async_computation.2 | async-start | bytes 524288 | tf_op jit(solution)/shard_map/psum | solution.py:92
  331.6 7.2 %copy-start.3 = (f32[4,4096]{1,0:T(4,128)S(1)}, f32[4,4096]{1,0:T(4,128)}, u32[]{:S(2)}) copy-start(f32[4,4096]{1,0:T(4,128)} %param.11) | copy-start | bytes 196612
  331.6 7.3 %copy-start.4 = (s32[4096]{0:T(1024)S(1)}, s32[4096]{0:T(1024)}, u32[]{:S(2)}) copy-start(s32[4096]{0:T(1024)} %param.10) | copy-start | bytes 49156
  331.6 135.2 %all-to-all-start = ((f32[32,16,4,4,256]{4,0,3,2,1:T(8,128)}), f32[32,16,4,4,256]{4,0,3,2,1:T(8,128)}, u32[]{:S(2)}, u32[]{:S(2)}) async-start(f32[32,16,4,4,256]{4,0,3,2,1:T(8,128)} %select_multiply_fusion), calls=%async_computation | async-start | bytes 16777216 | tf_op jit(solution)/shard_map/all_to_all | solution.py:97
Sparse Core Ops, SparseCore 0:
  46.4 61.4 all-reduce.8
  113.7 59.4 all-reduce.14
  179.1 59.4 all-reduce.12
  244.5 59.5 all-reduce.10
where the time goes:
time: 527 us
  waiting for transfers between devices  372 us (71%)
  other arithmetic  91.8 us (17%)
  local copies, waits for them, and re-layouts  37.1 us (7%)
  between operations  13.3 us (3%)
  starting transfers between devices  12.3 us (2%)
    psum x3, waiting for transfers between devices, body(): total_all, weighted_all = lax.psum((weight_total, weighted), 'ang')  178 us
    all_to_all x1, waiting for transfers between devices, body(): lax.all_to_all(picked, 'det', split_axis=1, concat_axis=4, tiled=True)  128 us
    psum x1, waiting for transfers between devices, body(): gain_map = lax.psum(jnp.sum(detail, axis=0), 'ang') / angles  61.3 us
    reshape x1, other arithmetic, body(): return moved.reshape(ang_dev, MOST, RB, total_cols)  36.4 us
    reduce_sum x1, other arithmetic, body(): gain_map = lax.psum(jnp.sum(detail, axis=0), 'ang') / angles  19.3 us
    reduce_sum x3, other arithmetic, body(): weight_total = jnp.sum(weights, axis=0)  14.4 us
    reshape x1, local copies, waits for them, and re-layouts, body(): return moved.reshape(ang_dev, MOST, RB, total_cols)  12.2 us
  transfers between devices with their start and end apart: 7, of which 7 were waited for; matrix products, arithmetic and copies ran while one was open for 0% of the time, Pallas kernels for 0%

commit v1 on v0

--- a/solution.py
+++ b/solution.py
@@ -94,7 +94,10 @@
     corrected = projected - gain_map
     picked = slot_blocks(corrected, destinations, owners)
     relative_all = band_offsets - jnp.arange(total_cols, dtype=jnp.int32)
-    arrived = lax.all_to_all(picked, "det", split_axis=1, concat_axis=4, tiled=True)
+    size = lax.axis_size("det")
+    pieces = jnp.stack(jnp.split(picked, size, axis=1), axis=0)
+    pieces = lax.all_to_all(pieces, "det", split_axis=0, concat_axis=0)
+    arrived = jnp.concatenate(pieces, axis=4)
     pad_widths = [(0, 0)] * (arrived.ndim - 1) + [(HB, HB)]
     widened_all = jnp.pad(arrived, pad_widths)
     moved = band_sum(widened_all, relative_all, band_weights, arrived.shape[-1])

time: 527 us -> 537 us (1.019)
  local copies, waits for them, and re-layouts: 37.1 us -> 50.4 us
    unnamed x14 -> x29, local copies, waits for them, and re-layouts: 7.55 us -> 20 us
where the time goes in v1:
time: 537 us; the launch traced here: 536 us
  waiting for transfers between devices  372 us (69%)
  other arithmetic  87.8 us (16%)
  local copies, waits for them, and re-layouts  50.4 us (9%)
  between operations  13.3 us (2%)
  starting transfers between devices  12.3 us (2%)
    psum x3, waiting for transfers between devices, body(): total_all, weighted_all = lax.psum((weight_total, weighted), 'ang')  178 us
    all_to_all x1, waiting for transfers between devices, body(): pieces = lax.all_to_all(pieces, 'det', split_axis=0, concat_axis=0)  128 us
    psum x1, waiting for transfers between devices, body(): gain_map = lax.psum(jnp.sum(detail, axis=0), 'ang') / angles  61.3 us
    reshape x1, other arithmetic, body(): return moved.reshape(ang_dev, MOST, RB, total_cols)  36.4 us
    unnamed x29, local copies, waits for them, and re-layouts  20 us
    reduce_sum x1, other arithmetic, body(): gain_map = lax.psum(jnp.sum(detail, axis=0), 'ang') / angles  19.3 us
    reduce_sum x3, other arithmetic, body(): weight_total = jnp.sum(weights, axis=0)  14.4 us
    reshape x1, local copies, waits for them, and re-layouts, body(): return moved.reshape(ang_dev, MOST, RB, total_cols)  12.2 us
  transfers between devices with their start and end apart: 7, of which 7 were waited for; matrix products, arithmetic and copies ran while one was open for 0% of the time, Pallas kernels for 0%

profile of v1, /device:TPU:6, one launch (start us, length us, event | category | flops | bytes accessed | tf_op | source)
XLA Modules:
  0.0 535.9 jit_solution(1971352100251218978)
XLA Ops:
  6.5 5.5 %copy.34 = f32[32,128,256]{1,0,2:T(8,128)} copy(f32[32,128,256]{2,1,0:T(8,128)} %param.6) | data formatting | bytes 8388608 | tf_op args[0]
  12.2 3.0 log_negate_fusion
  15.3 2.0 copy-done
  17.3 3.5 collective-permute-start
  20.7 1.3 collective-permute-start.1
  22.6 4.3 collective-permute-done.1
  26.9 19.3 %fusion.52 = (f32[128,256]{0,1:T(8,128)}, f32[32,128,256]{1,0,2:T(8,128)}) fusion(f32[32,128,256]{1,0,2:T(8,128)} %copy-done, f32[256]{0:T(256)S(1)} %add_convert_fusion, f32[32,128,4]{1,0,2:T(8,128)S(1)} %collective-permute-done.1, f32[32,128,4]{1,0,2:T(8,128)S(1)} %collective-permute-done), kind=kLoop, calls=%fused_computation.144 | loop fusion | flops 19890176 | bytes 8651776 | tf_op jit(solution)/shard_map/reduce_sum | solution.py:86
  46.4 61.3 %all-reduce.9.cloned.1.call-done = f32[128,256]{0,1:T(8,128)} async-done(((f32[128,256]{0,1:T(8,128)}), f32[128,256]{0,1:T(8,128)}) %all-reduce.9.cloned.1.call-update) | async-done | bytes 131088 | tf_op jit(solution)/shard_map/psum | solution.py:86
  107.8 0.9 broadcast_multiply_fusion
  108.7 4.8 fusion.29
  114.0 59.1 %all-reduce.15.cloned.1.call-done = (f32[128,256]{0,1:T(8,128)}, f32[128,256]{0,1:T(8,128)}) async-done(((f32[128,256]{0,1:T(8,128)}, f32[128,256]{0,1:T(8,128)}), (f32[128,256]{0,1:T(8,128)}, f32[128,256]{0,1:T(8,128)})) %all-reduce.15.cloned.1.call-update) | async-done | bytes 262160 | tf_op jit(solution)/shard_map/psum | solution.py:92
  173.1 1.0 div.57
  174.1 4.8 fusion.30
  179.2 59.4 %all-reduce.13.cloned.1.call-done = (f32[128,256]{0,1:T(8,128)}, f32[128,256]{0,1:T(8,128)}) async-done(((f32[128,256]{0,1:T(8,128)}, f32[128,256]{0,1:T(8,128)}), (f32[128,256]{0,1:T(8,128)}, f32[128,256]{0,1:T(8,128)})) %all-reduce.13.cloned.1.call-update) | async-done | bytes 262160 | tf_op jit(solution)/shard_map/psum | solution.py:92
  238.6 1.0 div.60
  239.6 4.8 fusion.31
  244.6 59.5 %all-reduce.11.cloned.1.call-done = (f32[128,256]{0,1:T(8,128)}, f32[128,256]{0,1:T(8,128)}) async-done(((f32[128,256]{0,1:T(8,128)}, f32[128,256]{0,1:T(8,128)}), (f32[128,256]{0,1:T(8,128)}, f32[128,256]{0,1:T(8,128)})) %all-reduce.11.cloned.1.call-update) | async-done | bytes 262160 | tf_op jit(solution)/shard_map/psum | solution.py:92
  304.1 1.0 div.63
  305.1 5.4 %broadcast_subtract_fusion = f32[32,128,256]{1,0,2:T(8,128)} fusion(f32[128,256]{0,1:T(8,128)S(1)} %div.63, f32[128,256]{0,1:T(8,128)S(1)} %copy.35, f32[32,128,256]{1,0,2:T(8,128)} %copy.34, f32[128,256]{0,1:T(8,128)S(1)} %copy.33), kind=kLoop, calls=%fused_computation.59 | loop fusion | flops 4194304 | bytes 8781824 | tf_op jit(solution)/shard_map/sub | solution.py:94
  310.5 5.6 %copy.36 = f32[32,128,256]{2,0,1:T(8,128)} copy(f32[32,128,256]{1,0,2:T(8,128)} %broadcast_subtract_fusion) | data formatting | bytes 8388608 | tf_op jit(solution)/shard_map/sub | solution.py:94
  316.1 6.7 %gather_fusion = f32[64,32,4,256]{3,1,2,0:T(8,128)} fusion(f32[32,32,4,256]{3,0,2,1:T(8,128)} %bitcast.80, s32[1024]{0:T(1024)S(1)} %pad_clamp_fusion), kind=kCustom, calls=%fused_computation | custom fusion | bytes 16777472 | tf_op jit(solution)/shard_map/jit(_take)/gather | solution.py:72
  322.8 4.9 select_multiply_fusion
  327.7 0.8 fusion.47
  331.8 0.8 fusion.42
  334.3 0.8 fusion.39
  336.8 0.8 fusion.36
  338.5 0.8 fusion.34
  341.0 7.2 %all-to-all-start = ((f32[16,32,1,4,4,256]{5,1,4,3,2,0:T(8,128)}), f32[16,32,1,4,4,256]{5,1,4,3,2,0:T(8,128)}, u32[]{:S(2)}, u32[]{:S(2)}) async-start(f32[16,32,1,4,4,256]{5,1,4,3,2,0:T(8,128)} %fusion.32), calls=%async_computation | async-start | bytes 16777216 | tf_op jit(solution)/shard_map/all_to_all | solution.py:99
  348.3 127.9 %all-to-all-done = f32[16,32,1,4,4,256]{5,1,4,3,2,0:T(8,128)} async-done(((f32[16,32,1,4,4,256]{5,1,4,3,2,0:T(8,128)}), f32[16,32,1,4,4,256]{5,1,4,3,2,0:T(8,128)}, u32[]{:S(2)}, u32[]{:S(2)}) %all-to-all-start) | async-done | bytes 8388640 | tf_op jit(solution)/shard_map/all_to_all | solution.py:99
  476.2 4.6 copy.41
  480.8 36.4 %add_bitcast_fusion = f32[32,4,4,4096]{3,0,2,1:T(8,128)} fusion(f32[32,1,4,4,4096]{4,0,3,2,1:T(8,128)S(1)} %bitcast.81, f32[4096]{0:T(1024)S(1)} %get-tuple-element.24, f32[4096]{0:T(1024)S(1)} %get-tuple-element.25, f32[4096]{0:T(1024)S(1)} %get-tuple-element.26, f32[4096]{0:T(1024)S(1)} %get-tuple-element.27, f32[4096]{0:T(1024)S(1)} %get-tuple-element.28, ...), kind=kLoop, calls=%fused_computation.1 | loop fusion | flops 69206016 | bytes 17055744 | tf_op jit(solution)/shard_map/reshape | solution.py:104
  517.2 12.2 %copy.40 = f32[32,4,4,4096]{3,2,1,0:T(4,128)} copy(f32[32,4,4,4096]{3,0,2,1:T(8,128)} %add_bitcast_fusion) | data formatting | bytes 16777216 | tf_op jit(solution)/shard_map/reshape | solution.py:104
  (50 shorter events, 11.2 us)
Async XLA Ops:
  6.5 5.5 %copy-start.1 = (f32[128,256]{1,0:T(8,128)S(1)}, f32[128,256]{1,0:T(8,128)}, u32[]{:S(2)}) copy-start(f32[128,256]{1,0:T(8,128)} %param.7) | copy-start | bytes 393220
  6.5 5.6 %copy-start.2 = (f32[128,256]{1,0:T(8,128)S(1)}, f32[128,256]{1,0:T(8,128)}, u32[]{:S(2)}) copy-start(f32[128,256]{1,0:T(8,128)} %param.8) | copy-start | bytes 393220
  6.5 15.5 %copy-start.5 = (s32[32,1]{0,1:T(1,128)S(1)}, s32[32,1]{0,1:T(1,128)}, u32[]{:S(2)}) copy-start(s32[32,1]{0,1:T(1,128)} %param.9) | copy-start | bytes 388
  6.5 101.2 %all-reduce.9.cloned.1.call-start = ((), (), s32[]{:S(2)}) async-start(), calls=%async_computation.1 | async-start | bytes 262144 | tf_op jit(solution)/shard_map/psum | solution.py:86
  15.3 2.0 copy-start
  17.3 5.4 %collective-permute-start = (f32[32,128,4]{1,0,2:T(8,128)S(1)}, f32[32,128,4]{1,0,2:T(8,128)S(1)}, u32[]{:S(2)}, u32[]{:S(2)}) collective-permute-start(f32[32,128,4]{1,0,2:T(8,128)S(1)} %get-tuple-element.21), channel_id=1, source_target_pairs={{0,1},{1,2},{2,3},{3,4},{4,5},{5,6},{6,7},{7,8},{8,9},{9,10},{10,1... | collective-permute-start | bytes 196616 | tf_op jit(solution)/shard_map/ppermute | solution.py:22
  20.7 6.2 %collective-permute-start.1 = (f32[32,128,4]{1,0,2:T(8,128)S(1)}, f32[32,128,4]{1,0,2:T(8,128)S(1)}, u32[]{:S(2)}, u32[]{:S(2)}) collective-permute-start(f32[32,128,4]{1,0,2:T(8,128)S(1)} %get-tuple-element.22), channel_id=1, source_target_pairs={{1,0},{2,1},{3,2},{4,3},{5,4},{6,5},{7,6},{8,7},{9,8},{10,9},{11,1... | collective-permute-start | bytes 196616 | tf_op jit(solution)/shard_map/ppermute | solution.py:23
  46.2 126.9 %all-reduce.15.cloned.1.call-start = ((), (), s32[]{:S(2)}) async-start(), calls=%async_computation.4 | async-start | bytes 524288 | tf_op jit(solution)/shard_map/psum | solution.py:92
  113.5 125.0 %all-reduce.13.cloned.1.call-start = ((), (), s32[]{:S(2)}) async-start(), calls=%async_computation.3 | async-start | bytes 524288 | tf_op jit(solution)/shard_map/psum | solution.py:92
  178.9 125.1 %all-reduce.11.cloned.1.call-start = ((), (), s32[]{:S(2)}) async-start(), calls=%async_computation.2 | async-start | bytes 524288 | tf_op jit(solution)/shard_map/psum | solution.py:92
  341.0 7.2 %copy-start.3 = (f32[4,4096]{1,0:T(4,128)S(1)}, f32[4,4096]{1,0:T(4,128)}, u32[]{:S(2)}) copy-start(f32[4,4096]{1,0:T(4,128)} %param.11) | copy-start | bytes 196612
  341.0 7.3 %copy-start.4 = (s32[4096]{0:T(1024)S(1)}, s32[4096]{0:T(1024)}, u32[]{:S(2)}) copy-start(s32[4096]{0:T(1024)} %param.10) | copy-start | bytes 49156
  341.0 135.2 %all-to-all-start = ((f32[16,32,1,4,4,256]{5,1,4,3,2,0:T(8,128)}), f32[16,32,1,4,4,256]{5,1,4,3,2,0:T(8,128)}, u32[]{:S(2)}, u32[]{:S(2)}) async-start(f32[16,32,1,4,4,256]{5,1,4,3,2,0:T(8,128)} %fusion.32), calls=%async_computation | async-start | bytes 16777216 | tf_op jit(solution)/shard_map/all_to_all | solution.py:99
Sparse Core Ops, SparseCore 0:
  46.3 61.4 all-reduce.8
  113.7 59.4 all-reduce.14
  179.1 59.4 all-reduce.12
  244.5 59.5 all-reduce.10
